TPU v7x, 32 devices: a whole 2x2x4 slice. The times are simulated.
32 devices in a mesh: space: 16 (over z, y, x), mem: 2 (over core).
Axes of the slice: x: 2, y: 2, z: 4, core: 2. Of those that a mesh axis runs over, the one named last changes fastest.
Arguments:
- perturb: float32 [1024, 4096], P(('space', 'mem')), may hold values from -6 to 6
- pair_list: int32 [64, 3], P('space'), may hold values from 0 to 15, as said below
- pair_count: int32 [16], P('space'), may hold values from 1 to 4, as said below
- band_weight: float32 [8], replicated, may hold values from 0.25 to 1
- cov_scale: float32 [1], replicated, may hold values from 0.5 to 2
- target: float32 [4096, 1024], P('space', 'mem'), may hold values from -6 to 6
- first_guess: float32 [4096, 1024], P('space', 'mem'), may hold values from -6 to 6
Outputs:
- solution: float32 [4096, 1024], P('space', 'mem')
Inputs may be any that keep to these rules, and one draw needn't show every extreme that they name: `pair_list`: rows 4 * s to 4 * s + 3 are owner s's slots. The first block of each is owner s's own block s; the second is the first plus d modulo 16, with 0 <= d <= 3; each of the four pairs (d = 0 to 3) stands in exactly one slot of its owner. The third column is an index into band_weight. Only the first pair_count[s] slots of owner s are live; in every draw some owner has all 4 slots live.
All inputs are finite; a program needn't handle non-finite values.
Results may differ from a plain program's by a relative error of at most 0.0003.
Values sent between devices are 32-bit elements; how exact they have to be, the bound alone decides.
A program may use at most 64 MiB of HBM per device.

v0:
```python
import jax
import jax.numpy as jnp
from jax import lax
from jax.sharding import PartitionSpec as P

BLOCK = 256
MEMBERS = 1024
REACH_DEV = 3
NBANDS = 8
ITERS = 2


def shifted(array, axis, by):
    count = lax.axis_size(axis)
    return lax.ppermute(array, axis, [(i, (i + by) % count) for i in range(count)])


def fetch_members(own_members):
    pieces = [own_members]
    for offset in range(1, REACH_DEV + 1):
        pieces.append(shifted(own_members, "space", -offset))
    return jnp.concatenate(pieces, axis=1)


def fetch_field(iterate):
    pieces = [iterate]
    for offset in range(1, REACH_DEV + 1):
        pieces.append(shifted(iterate, "space", -offset))
    return jnp.concatenate(pieces, axis=0)


def return_partials(pieces):
    total = pieces[0]
    for offset in range(1, REACH_DEV + 1):
        total = total + shifted(pieces[offset], "space", offset)
    return total


def per_device(perturb, pair_list, pair_count, band_weight, cov_scale, target, first_guess):
    own_members = lax.all_to_all(perturb, "space", split_axis=1, concat_axis=0, tiled=True)
    rows_dev = own_members.shape[1]
    blocks_dev = rows_dev // BLOCK
    blocks_near = (REACH_DEV + 1) * blocks_dev
    blocks_all = blocks_dev * lax.axis_size("space")
    slot_total = pair_list.shape[0]
    first_local = (pair_list[:, 0] - lax.axis_index("space") * blocks_dev) % blocks_all
    second_local = (pair_list[:, 1] - lax.axis_index("space") * blocks_dev) % blocks_all
    living = (jnp.arange(slot_total, dtype=jnp.int32) < pair_count[0]).astype(jnp.float32)
    band_table = (pair_list[:, 2][:, None] == jnp.arange(NBANDS, dtype=jnp.int32)[None, :]).astype(
        jnp.float32
    )
    band_now = jnp.dot(
        band_table, band_weight, precision=lax.Precision.HIGHEST, preferred_element_type=jnp.float32
    )
    weights = cov_scale[0] * band_now * living / (MEMBERS - 1)
    members_near = fetch_members(own_members)

    def build_tile(slot_pair):
        first_cols = lax.dynamic_slice_in_dim(members_near, slot_pair[0] * BLOCK, BLOCK, 1)
        second_cols = lax.dynamic_slice_in_dim(members_near, slot_pair[1] * BLOCK, BLOCK, 1)
        return jnp.einsum(
            "ma,mb->ab",
            first_cols,
            second_cols,
            precision=lax.Precision.HIGHEST,
            preferred_element_type=jnp.float32,
        )

    partial_value = (
        lax.map(build_tile, jnp.stack([first_local, second_local], 1)) * weights[:, None, None]
    )
    tiles = lax.psum(partial_value, "mem")
    block_ids = jnp.arange(blocks_near, dtype=jnp.int32)
    first_select = (first_local[:, None] == block_ids[None, :]).astype(jnp.float32)
    second_select = (second_local[:, None] == block_ids[None, :]).astype(jnp.float32)
    mirror_mask = (first_local != second_local).astype(jnp.float32)
    iterate = first_guess
    columns = iterate.shape[1]
    for sweep in range(ITERS):
        field_near = fetch_field(iterate).reshape(blocks_near, BLOCK, columns)
        near_blocks = jnp.take(field_near, second_local, axis=0)
        own_blocks = jnp.take(field_near, first_local, axis=0)
        forward = jnp.einsum(
            "pab,pbc->pac",
            tiles,
            near_blocks,
            precision=lax.Precision.HIGHEST,
            preferred_element_type=jnp.float32,
        )
        mirror = jnp.einsum(
            "pab,pac->pbc",
            tiles,
            own_blocks,
            precision=lax.Precision.HIGHEST,
            preferred_element_type=jnp.float32,
        )
        mirror = mirror * mirror_mask[:, None, None]
        collected = jnp.einsum(
            "pl,pac->lac",
            first_select,
            forward,
            precision=lax.Precision.HIGHEST,
            preferred_element_type=jnp.float32,
        )
        collected = collected + jnp.einsum(
            "pl,pac->lac",
            second_select,
            mirror,
            precision=lax.Precision.HIGHEST,
            preferred_element_type=jnp.float32,
        )
        applied = return_partials([collected[offset] for offset in range(REACH_DEV + 1)])
        iterate = iterate + 0.5 * (target - iterate - applied)
    return iterate


def solution(mesh):
    in_specs = (
        P(("space", "mem"), None),
        P("space", None),
        P("space"),
        P(),
        P(),
        P("space", "mem"),
        P("space", "mem"),
    )
    out_specs = P("space", "mem")
    return jax.shard_map(
        per_device, mesh=mesh, in_specs=in_specs, out_specs=out_specs, check_vma=False
    )
```

profile of v0, /device:TPU:2, one launch (start us, length us, event | category | flops | bytes accessed | tf_op | source)
XLA Modules:
  0.0 288.0 jit_solution(15387314568821327748)
XLA Ops:
  6.5 1.9 copy.56
  8.5 7.3 %all-to-all-start = ((f32[32,16,256]{2,0,1:T(8,128)}), f32[32,16,256]{2,0,1:T(8,128)S(1)}, u32[]{:S(2)}, u32[]{:S(2)}) async-start(f32[32,16,256]{2,0,1:T(8,128)} %bitcast.87), calls=%async_computation | async-start | bytes 1048576 | tf_op jit(solution)/shard_map/all_to_all | solution.py:40
  15.9 4.2 %collective-permute-start.4 = (f32[256,512]{1,0:T(8,128)S(1)}, f32[256,512]{1,0:T(8,128)}, u32[]{:S(2)}, u32[]{:S(2)}) collective-permute-start(f32[256,512]{1,0:T(8,128)S(1)} %copy-done.8), channel_id=1, source_target_pairs={{0,28},{2,30},{4,0},{6,2},{8,4},{10,6},{12,8},{14,10},{16,12},{18,... | collective-permute-start | bytes 1572872 | tf_op jit(solution)/shard_map/ppermute | solution.py:15
  20.1 0.6 collective-permute-start.3
  21.9 0.2 slice_reduce_fusion
  22.1 0.1 copy.21
  22.2 0.1 copy.22
  22.4 7.6 %all-to-all-done = f32[32,16,256]{2,0,1:T(8,128)S(1)} async-done(((f32[32,16,256]{2,0,1:T(8,128)}), f32[32,16,256]{2,0,1:T(8,128)S(1)}, u32[]{:S(2)}, u32[]{:S(2)}) %all-to-all-start) | async-done | bytes 524320 | tf_op jit(solution)/shard_map/all_to_all | solution.py:40
  29.9 23.3 %collective-permute-start.2 = (f32[512,256]{1,0:T(8,128)S(1)}, f32[512,256]{1,0:T(8,128)S(1)}, u32[]{:S(2)}, u32[]{:S(2)}) collective-permute-start(f32[512,256]{1,0:T(8,128)S(1)} %bitcast.103), channel_id=1, source_target_pairs={{0,26},{2,28},{4,30},{6,0},{8,2},{10,4},{12,6},{14,8},{16,10},{18,... | collective-permute-start | bytes 1572872 | tf_op jit(solution)/shard_map/ppermute | solution.py:15
  53.3 1.8 collective-permute-start.1
  55.0 1.3 collective-permute-start
  56.3 0.2 fusion.23
  56.6 9.0 %collective-permute-done.2 = f32[512,256]{1,0:T(8,128)S(1)} collective-permute-done((f32[512,256]{1,0:T(8,128)S(1)}, f32[512,256]{1,0:T(8,128)S(1)}, u32[]{:S(2)}, u32[]{:S(2)}) %collective-permute-start.2) | collective-permute-done | bytes 524320 | tf_op jit(solution)/shard_map/ppermute | solution.py:15
  65.6 6.2 %collective-permute-start.5 = (f32[256,512]{1,0:T(8,128)S(1)}, f32[256,512]{1,0:T(8,128)}, u32[]{:S(2)}, u32[]{:S(2)}) collective-permute-start(f32[256,512]{1,0:T(8,128)S(1)} %copy-done.8), channel_id=1, source_target_pairs={{0,26},{2,28},{4,30},{6,0},{8,2},{10,4},{12,6},{14,8},{16,10},{18,... | collective-permute-start | bytes 1572872 | tf_op jit(solution)/shard_map/ppermute | solution.py:15
  71.8 4.9 %collective-permute-done.1 = f32[512,256]{1,0:T(8,128)S(1)} collective-permute-done((f32[512,256]{1,0:T(8,128)S(1)}, f32[512,256]{1,0:T(8,128)S(1)}, u32[]{:S(2)}, u32[]{:S(2)}) %collective-permute-start.1) | collective-permute-done | bytes 524320 | tf_op jit(solution)/shard_map/ppermute | solution.py:15
  76.7 3.1 %collective-permute-done = f32[512,256]{1,0:T(8,128)S(1)} collective-permute-done((f32[512,256]{1,0:T(8,128)S(1)}, f32[512,256]{1,0:T(8,128)S(1)}, u32[]{:S(2)}, u32[]{:S(2)}) %collective-permute-start) | collective-permute-done | bytes 524320 | tf_op jit(solution)/shard_map/ppermute | solution.py:15
  79.9 0.3 pad_maximum_fusion
  80.1 15.1 %while.10 = (s32[]{:T(128)}, f32[4,256,256]{2,1,0:T(8,128)}, s32[4,2]{0,1:T(2,128)S(1)}, f32[512,1024]{1,0:T(8,128)S(1)}, s32[]{:T(128)}, /*index=5*/s32[1,1]{0,1:T(1,128)}, s32[]{:T(128)}, s32[]{:T(128)}) while((s32[]{:T(128)}, f32[4,256,256]{2,1,0:T(8,128)}, s32[4,2]{0,1:T(2,128)S(1)}, f32[512,1024]{1,0:T(8,128)S(1)}, s32[]{:T(128)}, ...), condition=%wide.region_1.2_spmd, body=%wide.region_0.1_spmd.sunk | while | flops 402653184 | bytes 1310953 | solution.py:70
  80.1 0.1 constant_dynamic-slice_fusion.2
  80.2 0.6 fusion.78
  82.2 1.7 fusion.79
  84.0 0.6 fusion.78
  85.9 1.8 fusion.79
  87.7 0.6 fusion.78
  89.7 1.8 fusion.79
  91.5 0.6 fusion.78
  93.5 1.8 fusion.79
  95.2 2.4 broadcast_multiply_fusion
  97.7 3.7 %collective-permute-done.5 = f32[256,512]{1,0:T(8,128)} collective-permute-done((f32[256,512]{1,0:T(8,128)S(1)}, f32[256,512]{1,0:T(8,128)}, u32[]{:S(2)}, u32[]{:S(2)}) %collective-permute-start.5) | collective-permute-done | bytes 524320 | tf_op jit(solution)/shard_map/ppermute | solution.py:15
  101.4 1.6 pad_maximum_fusion.1
  103.0 2.0 gather_fusion.1
  105.0 2.0 gather_fusion
  107.1 26.6 %all-reduce.2.cloned.1.call-done = f32[4,256,256]{2,1,0:T(8,128)} async-done(((f32[4,256,256]{2,1,0:T(8,128)}), f32[4,256,256]{2,1,0:T(8,128)}) %all-reduce.2.cloned.1.call-update) | async-done | bytes 1048592 | tf_op jit(solution)/shard_map/psum | solution.py:72
  133.7 4.2 %fusion.14 = f32[4,256,512]{2,1,0:T(8,128)S(1)} fusion(f32[4,256,256]{2,1,0:T(8,128)} %all-reduce.2.cloned.1.call-done, f32[4,256,512]{2,1,0:T(8,128)} %gather_fusion.1, pred[4]{0:T(512)(128)(4,1)S(1)} %compare_and_fusion), kind=kOutput, calls=%fused_computation.26 | convolution fusion | flops 1611137024 | bytes 5242884 | tf_op jit(solution)/shard_map/pab,pac->pbc/dot_general | solution.py:90
  137.9 3.3 %fusion.7 = f32[4,256,512]{2,0,1:T(4,128)S(1)} fusion(f32[4,256,512]{2,1,0:T(8,128)S(1)} %fusion.14, f32[4]{0:T(128)S(1)} %get-tuple-element.39, s32[4]{0:T(128)S(1)} %bitcast.113), kind=kOutput, calls=%fused_computation.18 | convolution fusion | flops 25690128 | bytes 4194336 | tf_op jit(solution)/shard_map/pl,pac->lac/dot_general | solution.py:105
  141.3 2.1 fusion.16
  143.4 3.8 %fusion.18 = f32[4,256,512]{2,0,1:T(4,128)S(1)} fusion(f32[4,256,512]{2,0,1:T(4,128)S(1)} %fusion.7, f32[4,256,512]{2,1,0:T(8,128)S(1)} %fusion.16, s32[4]{0:T(128)S(1)} %bitcast.111), kind=kOutput, calls=%fused_computation.30 | convolution fusion | flops 25690128 | bytes 6291472 | tf_op jit(solution)/shard_map/pl,pac->lac/dot_general | solution.py:98
  147.2 1.5 fusion.67
  148.9 1.5 collective-permute-start.7
  150.4 1.5 collective-permute-start.8
  151.9 2.4 collective-permute-start.6
  154.2 19.0 %collective-permute-done.7 = f32[256,512]{1,0:T(8,128)S(1)} collective-permute-done((f32[256,512]{1,0:T(8,128)S(1)}, f32[256,512]{1,0:T(8,128)S(1)}, u32[]{:S(2)}, u32[]{:S(2)}) %collective-permute-start.7) | collective-permute-done | bytes 524320 | tf_op jit(solution)/shard_map/ppermute | solution.py:15
  173.3 3.7 %collective-permute-done.8 = f32[256,512]{1,0:T(8,128)S(1)} collective-permute-done((f32[256,512]{1,0:T(8,128)S(1)}, f32[256,512]{1,0:T(8,128)S(1)}, u32[]{:S(2)}, u32[]{:S(2)}) %collective-permute-start.8) | collective-permute-done | bytes 524320 | tf_op jit(solution)/shard_map/ppermute | solution.py:15
  177.0 0.4 fusion.45
  177.3 3.7 %collective-permute-start.11 = (f32[256,512]{1,0:T(8,128)S(1)}, f32[256,512]{1,0:T(8,128)S(1)}, u32[]{:S(2)}, u32[]{:S(2)}) collective-permute-start(f32[256,512]{1,0:T(8,128)S(1)} %fusion.45), channel_id=1, source_target_pairs={{0,26},{2,28},{4,30},{6,0},{8,2},{10,4},{12,6},{14,8},{16,10},{18,... | collective-permute-start | bytes 1572872 | tf_op jit(solution)/shard_map/ppermute | solution.py:15
  181.0 11.5 %collective-permute-start.10 = (f32[256,512]{1,0:T(8,128)S(1)}, f32[256,512]{1,0:T(8,128)S(1)}, u32[]{:S(2)}, u32[]{:S(2)}) collective-permute-start(f32[256,512]{1,0:T(8,128)S(1)} %fusion.45), channel_id=1, source_target_pairs={{0,28},{2,30},{4,0},{6,2},{8,4},{10,6},{12,8},{14,10},{16,12},{18,... | collective-permute-start | bytes 1572872 | tf_op jit(solution)/shard_map/ppermute | solution.py:15
  192.5 9.5 %collective-permute-done.11 = f32[256,512]{1,0:T(8,128)S(1)} collective-permute-done((f32[256,512]{1,0:T(8,128)S(1)}, f32[256,512]{1,0:T(8,128)S(1)}, u32[]{:S(2)}, u32[]{:S(2)}) %collective-permute-start.11) | collective-permute-done | bytes 524320 | tf_op jit(solution)/shard_map/ppermute | solution.py:15
  202.0 12.0 %collective-permute-done.10 = f32[256,512]{1,0:T(8,128)S(1)} collective-permute-done((f32[256,512]{1,0:T(8,128)S(1)}, f32[256,512]{1,0:T(8,128)S(1)}, u32[]{:S(2)}, u32[]{:S(2)}) %collective-permute-start.10) | collective-permute-done | bytes 524320 | tf_op jit(solution)/shard_map/ppermute | solution.py:15
  214.0 0.2 pad_maximum_fusion.2
  214.2 2.0 gather_fusion.3
  216.2 2.0 gather_fusion.2
  218.2 4.0 %fusion.10 = f32[4,256,512]{2,1,0:T(8,128)S(1)} fusion(f32[4,256,256]{2,1,0:T(8,128)S(1)} %copy-done.1, f32[4,256,512]{2,1,0:T(8,128)} %gather_fusion.3, pred[4]{0:T(512)(128)(4,1)S(1)} %compare_and_fusion), kind=kOutput, calls=%fused_computation.22 | convolution fusion | flops 1611137024 | bytes 5242884 | tf_op jit(solution)/shard_map/pab,pac->pbc/dot_general | solution.py:90
  222.2 3.3 %fusion.4 = f32[4,256,512]{2,0,1:T(4,128)S(1)} fusion(f32[4,256,512]{2,1,0:T(8,128)S(1)} %fusion.10, f32[4]{0:T(128)S(1)} %get-tuple-element.39, s32[4]{0:T(128)S(1)} %bitcast.114), kind=kOutput, calls=%fused_computation.14 | convolution fusion | flops 25690128 | bytes 4194336 | tf_op jit(solution)/shard_map/pl,pac->lac/dot_general | solution.py:105
  225.6 2.1 fusion.12
  227.7 3.2 %fusion.5 = f32[4,256,512]{2,0,1:T(4,128)S(1)} fusion(f32[4,256,512]{2,1,0:T(8,128)S(1)} %fusion.12, s32[4]{0:T(128)S(1)} %bitcast.112), kind=kOutput, calls=%fused_computation.15 | convolution fusion | flops 25165840 | bytes 4194320 | tf_op jit(solution)/shard_map/pl,pac->lac/dot_general | solution.py:98
  231.0 1.2 copy_add_fusion
  232.2 0.1 slice_bitcast_fusion.2
  232.3 1.6 collective-permute-start.12
  233.9 7.3 %collective-permute-start.14 = (f32[256,512]{1,0:T(8,128)S(1)}, f32[256,512]{1,0:T(8,128)S(1)}, u32[]{:S(2)}, u32[]{:S(2)}) collective-permute-start(f32[256,512]{1,0:T(8,128)S(1)} %get-tuple-element.44), channel_id=1, source_target_pairs={{0,6},{2,8},{4,10},{6,12},{8,14},{10,16},{12,18},{14,20},{16,22},{... | collective-permute-start | bytes 1572872 | tf_op jit(solution)/shard_map/ppermute | solution.py:15
  241.2 4.8 %collective-permute-start.13 = (f32[256,512]{1,0:T(8,128)S(1)}, f32[256,512]{1,0:T(8,128)S(1)}, u32[]{:S(2)}, u32[]{:S(2)}) collective-permute-start(f32[256,512]{1,0:T(8,128)S(1)} %get-tuple-element.45), channel_id=1, source_target_pairs={{0,4},{2,6},{4,8},{6,10},{8,12},{10,14},{12,16},{14,18},{16,20},{1... | collective-permute-start | bytes 1572872 | tf_op jit(solution)/shard_map/ppermute | solution.py:15
  246.0 8.8 %collective-permute-done.12 = f32[256,512]{1,0:T(8,128)S(1)} collective-permute-done((f32[256,512]{1,0:T(8,128)S(1)}, f32[256,512]{1,0:T(8,128)S(1)}, u32[]{:S(2)}, u32[]{:S(2)}) %collective-permute-start.12) | collective-permute-done | bytes 524320 | tf_op jit(solution)/shard_map/ppermute | solution.py:15
  254.8 6.1 %collective-permute-done.14 = f32[256,512]{1,0:T(8,128)S(1)} collective-permute-done((f32[256,512]{1,0:T(8,128)S(1)}, f32[256,512]{1,0:T(8,128)S(1)}, u32[]{:S(2)}, u32[]{:S(2)}) %collective-permute-start.14) | collective-permute-done | bytes 524320 | tf_op jit(solution)/shard_map/ppermute | solution.py:15
  260.9 19.1 %collective-permute-done.13 = f32[256,512]{1,0:T(8,128)S(1)} collective-permute-done((f32[256,512]{1,0:T(8,128)S(1)}, f32[256,512]{1,0:T(8,128)S(1)}, u32[]{:S(2)}, u32[]{:S(2)}) %collective-permute-start.13) | collective-permute-done | bytes 524320 | tf_op jit(solution)/shard_map/ppermute | solution.py:15
  280.0 1.2 fusion.39
  (43 shorter events, 0.5 us)
Async XLA Ops:
  6.5 49.8 %copy-start = (f32[8]{0:T(128)S(1)}, f32[8]{0:T(128)}, u32[]{:S(2)}) copy-start(f32[8]{0:T(128)} %param.14) | copy-start | bytes 100
  6.5 9.3 %copy-start.8 = (f32[256,512]{1,0:T(8,128)S(1)}, f32[256,512]{1,0:T(8,128)}, u32[]{:S(2)}) copy-start(f32[256,512]{1,0:T(8,128)} %param.17) | copy-start | bytes 1572868
  6.5 15.4 %copy-start.9 = (s32[4,3]{1,0:T(4,128)S(1)}, s32[4,3]{1,0:T(4,128)}, u32[]{:S(2)}) copy-start(s32[4,3]{1,0:T(4,128)} %param.12) | copy-start | bytes 148
  8.5 21.4 %all-to-all-start = ((f32[32,16,256]{2,0,1:T(8,128)}), f32[32,16,256]{2,0,1:T(8,128)S(1)}, u32[]{:S(2)}, u32[]{:S(2)}) async-start(f32[32,16,256]{2,0,1:T(8,128)} %bitcast.87), calls=%async_computation | async-start | bytes 1048576 | tf_op jit(solution)/shard_map/all_to_all | solution.py:40
  15.8 117.9 %all-reduce.2.cloned.1.call-start = ((), (), s32[]{:S(2)}) async-start(), calls=%async_computation.1 | async-start | bytes 2097152 | tf_op jit(solution)/shard_map/psum | solution.py:72
  15.9 81.9 %collective-permute-start.4 = (f32[256,512]{1,0:T(8,128)S(1)}, f32[256,512]{1,0:T(8,128)}, u32[]{:S(2)}, u32[]{:S(2)}) collective-permute-start(f32[256,512]{1,0:T(8,128)S(1)} %copy-done.8), channel_id=1, source_target_pairs={{0,28},{2,30},{4,0},{6,2},{8,4},{10,6},{12,8},{14,10},{16,12},{18,... | collective-permute-start | bytes 1572872 | tf_op jit(solution)/shard_map/ppermute | solution.py:15
  20.1 77.6 %collective-permute-start.3 = (f32[256,512]{1,0:T(8,128)S(1)}, f32[256,512]{1,0:T(8,128)}, u32[]{:S(2)}, u32[]{:S(2)}) collective-permute-start(f32[256,512]{1,0:T(8,128)S(1)} %copy-done.8), channel_id=1, source_target_pairs={{0,30},{2,0},{4,2},{6,4},{8,6},{10,8},{12,10},{14,12},{16,14},{18,... | collective-permute-start | bytes 1572872 | tf_op jit(solution)/shard_map/ppermute | solution.py:15
  29.9 35.7 %collective-permute-start.2 = (f32[512,256]{1,0:T(8,128)S(1)}, f32[512,256]{1,0:T(8,128)S(1)}, u32[]{:S(2)}, u32[]{:S(2)}) collective-permute-start(f32[512,256]{1,0:T(8,128)S(1)} %bitcast.103), channel_id=1, source_target_pairs={{0,26},{2,28},{4,30},{6,0},{8,2},{10,4},{12,6},{14,8},{16,10},{18,... | collective-permute-start | bytes 1572872 | tf_op jit(solution)/shard_map/ppermute | solution.py:15
  53.3 23.5 %collective-permute-start.1 = (f32[512,256]{1,0:T(8,128)S(1)}, f32[512,256]{1,0:T(8,128)S(1)}, u32[]{:S(2)}, u32[]{:S(2)}) collective-permute-start(f32[512,256]{1,0:T(8,128)S(1)} %bitcast.104), channel_id=1, source_target_pairs={{0,28},{2,30},{4,0},{6,2},{8,4},{10,6},{12,8},{14,10},{16,12},{18,... | collective-permute-start | bytes 1572872 | tf_op jit(solution)/shard_map/ppermute | solution.py:15
  55.0 24.8 %collective-permute-start = (f32[512,256]{1,0:T(8,128)S(1)}, f32[512,256]{1,0:T(8,128)S(1)}, u32[]{:S(2)}, u32[]{:S(2)}) collective-permute-start(f32[512,256]{1,0:T(8,128)S(1)} %bitcast.105), channel_id=1, source_target_pairs={{0,30},{2,0},{4,2},{6,4},{8,6},{10,8},{12,10},{14,12},{16,14},{18,... | collective-permute-start | bytes 1572872 | tf_op jit(solution)/shard_map/ppermute | solution.py:15
  65.6 35.9 %collective-permute-start.5 = (f32[256,512]{1,0:T(8,128)S(1)}, f32[256,512]{1,0:T(8,128)}, u32[]{:S(2)}, u32[]{:S(2)}) collective-permute-start(f32[256,512]{1,0:T(8,128)S(1)} %copy-done.8), channel_id=1, source_target_pairs={{0,26},{2,28},{4,30},{6,0},{8,2},{10,4},{12,6},{14,8},{16,10},{18,... | collective-permute-start | bytes 1572872 | tf_op jit(solution)/shard_map/ppermute | solution.py:15
  137.9 3.4 %copy-start.1 = (f32[4,256,256]{2,1,0:T(8,128)S(1)}, f32[4,256,256]{2,1,0:T(8,128)}, u32[]{:S(2)}) copy-start(f32[4,256,256]{2,1,0:T(8,128)} %all-reduce.2.cloned.1.call-done) | copy-start | bytes 3145732
  137.9 3.4 %copy-start.2 = (f32[4,256,512]{2,1,0:T(8,128)S(1)}, f32[4,256,512]{2,1,0:T(8,128)}, u32[]{:S(2)}) copy-start(f32[4,256,512]{2,1,0:T(8,128)} %gather_fusion) | copy-start | bytes 6291460
  148.7 28.2 %copy-start.6 = (f32[256,512]{1,0:T(8,128)S(1)}, f32[256,512]{1,0:T(8,128)}, u32[]{:S(2)}) copy-start(f32[256,512]{1,0:T(8,128)} %param.16) | copy-start | bytes 1572868
  148.9 24.4 %collective-permute-start.7 = (f32[256,512]{1,0:T(8,128)S(1)}, f32[256,512]{1,0:T(8,128)S(1)}, u32[]{:S(2)}, u32[]{:S(2)}) collective-permute-start(f32[256,512]{1,0:T(8,128)S(1)} %bitcast.110), channel_id=1, source_target_pairs={{0,4},{2,6},{4,8},{6,10},{8,12},{10,14},{12,16},{14,18},{16,20},{1... | collective-permute-start | bytes 1572872 | tf_op jit(solution)/shard_map/ppermute | solution.py:15
  150.4 26.6 %collective-permute-start.8 = (f32[256,512]{1,0:T(8,128)S(1)}, f32[256,512]{1,0:T(8,128)S(1)}, u32[]{:S(2)}, u32[]{:S(2)}) collective-permute-start(f32[256,512]{1,0:T(8,128)S(1)} %bitcast.109), channel_id=1, source_target_pairs={{0,6},{2,8},{4,10},{6,12},{8,14},{10,16},{12,18},{14,20},{16,22},{... | collective-permute-start | bytes 1572872 | tf_op jit(solution)/shard_map/ppermute | solution.py:15
  151.9 25.1 %collective-permute-start.6 = (f32[256,512]{1,0:T(8,128)S(1)}, f32[256,512]{1,0:T(8,128)S(1)}, u32[]{:S(2)}, u32[]{:S(2)}) collective-permute-start(f32[256,512]{1,0:T(8,128)S(1)} %bitcast.108), channel_id=1, source_target_pairs={{0,2},{2,4},{4,6},{6,8},{8,10},{10,12},{12,14},{14,16},{16,18},{18... | collective-permute-start | bytes 1572872 | tf_op jit(solution)/shard_map/ppermute | solution.py:15
  177.3 36.9 %copy-start.4 = (f32[256,512]{1,0:T(8,128)}, f32[256,512]{1,0:T(8,128)S(1)}, u32[]{:S(2)}) copy-start(f32[256,512]{1,0:T(8,128)S(1)} %fusion.45) | copy-start | bytes 1572868
  177.3 24.7 %collective-permute-start.11 = (f32[256,512]{1,0:T(8,128)S(1)}, f32[256,512]{1,0:T(8,128)S(1)}, u32[]{:S(2)}, u32[]{:S(2)}) collective-permute-start(f32[256,512]{1,0:T(8,128)S(1)} %fusion.45), channel_id=1, source_target_pairs={{0,26},{2,28},{4,30},{6,0},{8,2},{10,4},{12,6},{14,8},{16,10},{18,... | collective-permute-start | bytes 1572872 | tf_op jit(solution)/shard_map/ppermute | solution.py:15
  181.0 33.0 %collective-permute-start.10 = (f32[256,512]{1,0:T(8,128)S(1)}, f32[256,512]{1,0:T(8,128)S(1)}, u32[]{:S(2)}, u32[]{:S(2)}) collective-permute-start(f32[256,512]{1,0:T(8,128)S(1)} %fusion.45), channel_id=1, source_target_pairs={{0,28},{2,30},{4,0},{6,2},{8,4},{10,6},{12,8},{14,10},{16,12},{18,... | collective-permute-start | bytes 1572872 | tf_op jit(solution)/shard_map/ppermute | solution.py:15
  192.5 21.5 %collective-permute-start.9 = (f32[256,512]{1,0:T(8,128)S(1)}, f32[256,512]{1,0:T(8,128)S(1)}, u32[]{:S(2)}, u32[]{:S(2)}) collective-permute-start(f32[256,512]{1,0:T(8,128)S(1)} %fusion.45), channel_id=1, source_target_pairs={{0,30},{2,0},{4,2},{6,4},{8,6},{10,8},{12,10},{14,12},{16,14},{18,... | collective-permute-start | bytes 1572872 | tf_op jit(solution)/shard_map/ppermute | solution.py:15
  222.2 3.4 %copy-start.3 = (f32[4,256,512]{2,1,0:T(8,128)S(1)}, f32[4,256,512]{2,1,0:T(8,128)}, u32[]{:S(2)}) copy-start(f32[4,256,512]{2,1,0:T(8,128)} %gather_fusion.2) | copy-start | bytes 6291460
  232.2 47.8 %copy-start.5 = (f32[256,512]{1,0:T(8,128)S(1)}, f32[256,512]{1,0:T(8,128)}, u32[]{:S(2)}) copy-start(f32[256,512]{1,0:T(8,128)} %copy-done.4) | copy-start | bytes 1572868
  232.2 47.8 %copy-start.7 = (f32[256,512]{1,0:T(8,128)S(1)}, f32[256,512]{1,0:T(8,128)}, u32[]{:S(2)}) copy-start(f32[256,512]{1,0:T(8,128)} %param.16) | copy-start | bytes 1572868
  232.3 22.4 %collective-permute-start.12 = (f32[256,512]{1,0:T(8,128)S(1)}, f32[256,512]{1,0:T(8,128)S(1)}, u32[]{:S(2)}, u32[]{:S(2)}) collective-permute-start(f32[256,512]{1,0:T(8,128)S(1)} %get-tuple-element.43), channel_id=1, source_target_pairs={{0,2},{2,4},{4,6},{6,8},{8,10},{10,12},{12,14},{14,16},{16,18},{18... | collective-permute-start | bytes 1572872 | tf_op jit(solution)/shard_map/ppermute | solution.py:15
  233.9 27.0 %collective-permute-start.14 = (f32[256,512]{1,0:T(8,128)S(1)}, f32[256,512]{1,0:T(8,128)S(1)}, u32[]{:S(2)}, u32[]{:S(2)}) collective-permute-start(f32[256,512]{1,0:T(8,128)S(1)} %get-tuple-element.44), channel_id=1, source_target_pairs={{0,6},{2,8},{4,10},{6,12},{8,14},{10,16},{12,18},{14,20},{16,22},{... | collective-permute-start | bytes 1572872 | tf_op jit(solution)/shard_map/ppermute | solution.py:15
  241.2 38.8 %collective-permute-start.13 = (f32[256,512]{1,0:T(8,128)S(1)}, f32[256,512]{1,0:T(8,128)S(1)}, u32[]{:S(2)}, u32[]{:S(2)}) collective-permute-start(f32[256,512]{1,0:T(8,128)S(1)} %get-tuple-element.45), channel_id=1, source_target_pairs={{0,4},{2,6},{4,8},{6,10},{8,12},{10,14},{12,16},{14,18},{16,20},{1... | collective-permute-start | bytes 1572872 | tf_op jit(solution)/shard_map/ppermute | solution.py:15
Sparse Core Ops, SparseCore 0:
  97.8 35.9 all-reduce.1
where the time goes:
time: 288 us
  waiting for transfers between devices  133 us (46%)
  starting transfers between devices  79 us (27%)
  matrix products  33.3 us (12%)
  between operations  15 us (5%)
  local copies, waits for them, and re-layouts  14.9 us (5%)
  other arithmetic  7.2 us (2%)
  loops' own time  5.42 us (2%)
    ppermute x15, waiting for transfers between devices, shifted(): lax.ppermute(array, axis, [(i, (i + by) % count) for i in range(count)])  99 us
    ppermute x15, starting transfers between devices, shifted(): lax.ppermute(array, axis, [(i, (i + by) % count) for i in range(count)])  71.7 us
    psum x1, waiting for transfers between devices, per_device(): tiles = lax.psum(partial_value, 'mem')  26.6 us
    dot_general x2, matrix products, per_device(): jnp.einsum('pab,pac->pbc', tiles, own_blocks, precision=lax.Precision.HIG...  8.13 us
    all_to_all x1, waiting for transfers between devices, per_device(): lax.all_to_all(perturb, 'space', split_axis=1, concat_axis=0, tiled=True)  7.55 us
    all_to_all x1, starting transfers between devices, per_device(): lax.all_to_all(perturb, 'space', split_axis=1, concat_axis=0, tiled=True)  7.31 us
    dot_general x2, matrix products, per_device(): jnp.einsum('pl,pac->lac', first_select, forward, precision=lax.Precision....  7.02 us
    dot_general x4, matrix products, build_tile(): jnp.einsum('ma,mb->ab', first_cols, second_cols, precision=lax.Precision....  7.01 us
  transfers between devices with their start and end apart: 17, of which 13 were waited for; matrix products, arithmetic and copies ran while one was open for 6% of the time, Pallas kernels for 0%

commit v1 on v0

--- a/solution.py
+++ b/solution.py
@@ -37,7 +37,12 @@
 
 
 def per_device(perturb, pair_list, pair_count, band_weight, cov_scale, target, first_guess):
-    own_members = lax.all_to_all(perturb, "space", split_axis=1, concat_axis=0, tiled=True)
+    own_members = jnp.concatenate(
+        lax.all_to_all(
+            jnp.stack(jnp.split(perturb, lax.axis_size("space"), axis=1)), "space", 0, 0
+        ),
+        axis=0,
+    )
     rows_dev = own_members.shape[1]
     blocks_dev = rows_dev // BLOCK
     blocks_near = (REACH_DEV + 1) * blocks_dev

time: 288 us -> 309 us (1.073)
  local copies, waits for them, and re-layouts: 14.9 us -> 34.7 us
    unnamed x25 -> x40, local copies, waits for them, and re-layouts: 0.34 us -> 21 us
where the time goes in v1:
time: 309 us; the launch traced here: 307 us
  waiting for transfers between devices  133 us (43%)
  starting transfers between devices  79 us (26%)
  local copies, waits for them, and re-layouts  34.7 us (11%)
  matrix products  33.2 us (11%)
  between operations  15 us (5%)
  other arithmetic  7.21 us (2%)
  loops' own time  4.95 us (2%)
    ppermute x15, waiting for transfers between devices, shifted(): lax.ppermute(array, axis, [(i, (i + by) % count) for i in range(count)])  99.7 us
    ppermute x15, starting transfers between devices, shifted(): lax.ppermute(array, axis, [(i, (i + by) % count) for i in range(count)])  71.7 us
    psum x1, waiting for transfers between devices, per_device(): tiles = lax.psum(partial_value, 'mem')  25.9 us
    unnamed x40, local copies, waits for them, and re-layouts  21 us
    dot_general x2, matrix products, per_device(): jnp.einsum('pab,pac->pbc', tiles, own_blocks, precision=lax.Precision.HIG...  8.13 us
    all_to_all x1, waiting for transfers between devices, per_device(): lax.all_to_all(jnp.stack(jnp.split(perturb, lax.axis_size('space'), axis=...  7.58 us
    all_to_all x1, starting transfers between devices, per_device(): lax.all_to_all(jnp.stack(jnp.split(perturb, lax.axis_size('space'), axis=...  7.31 us
    dot_general x2, matrix products, per_device(): jnp.einsum('pl,pac->lac', first_select, forward, precision=lax.Precision....  7.02 us
  transfers between devices with their start and end apart: 17, of which 13 were waited for; matrix products, arithmetic and copies ran while one was open for 6% of the time, Pallas kernels for 0%

profile of v1, /device:TPU:2, one launch (start us, length us, event | category | flops | bytes accessed | tf_op | source)
XLA Modules:
  0.0 307.3 jit_solution(348701280800497161)
XLA Ops:
  6.5 1.4 constant_dynamic-update-slice_fusion.15
  8.0 1.4 constant_dynamic-update-slice_fusion.14
  9.3 1.4 constant_dynamic-update-slice_fusion.13
  10.7 1.4 constant_dynamic-update-slice_fusion.12
  12.1 1.4 constant_dynamic-update-slice_fusion.11
  13.5 1.4 constant_dynamic-update-slice_fusion.10
  14.8 1.4 constant_dynamic-update-slice_fusion.9
  16.2 1.4 constant_dynamic-update-slice_fusion.8
  17.6 1.4 constant_dynamic-update-slice_fusion.7
  19.0 1.4 constant_dynamic-update-slice_fusion.6
  20.3 1.4 constant_dynamic-update-slice_fusion.5
  21.7 1.4 constant_dynamic-update-slice_fusion.4
  23.1 1.4 constant_dynamic-update-slice_fusion.3
  24.5 1.4 constant_dynamic-update-slice_fusion.2
  25.8 1.4 constant_dynamic-update-slice_fusion.1
  27.2 1.4 constant_dynamic-update-slice_fusion
  28.6 7.3 %all-to-all-start = ((f32[16,32,256]{2,1,0:T(8,128)}), f32[16,32,256]{2,1,0:T(8,128)S(1)}, u32[]{:S(2)}, u32[]{:S(2)}) async-start(f32[16,32,256]{2,1,0:T(8,128)} %constant_dynamic-update-slice_fusion), calls=%async_computation | async-start | bytes 1048576 | tf_op jit(solution)/shard_map/all_to_all | solution.py:41
  35.9 4.2 %collective-permute-start.4 = (f32[256,512]{1,0:T(8,128)S(1)}, f32[256,512]{1,0:T(8,128)}, u32[]{:S(2)}, u32[]{:S(2)}) collective-permute-start(f32[256,512]{1,0:T(8,128)S(1)} %copy-done.8), channel_id=1, source_target_pairs={{0,28},{2,30},{4,0},{6,2},{8,4},{10,6},{12,8},{14,10},{16,12},{18,... | collective-permute-start | bytes 1572872 | tf_op jit(solution)/shard_map/ppermute | solution.py:15
  42.4 7.6 %all-to-all-done = f32[16,32,256]{2,1,0:T(8,128)S(1)} async-done(((f32[16,32,256]{2,1,0:T(8,128)}), f32[16,32,256]{2,1,0:T(8,128)S(1)}, u32[]{:S(2)}, u32[]{:S(2)}) %all-to-all-start) | async-done | bytes 524320 | tf_op jit(solution)/shard_map/all_to_all | solution.py:41
  50.0 23.3 %collective-permute-start.2 = (f32[512,256]{1,0:T(8,128)S(1)}, f32[512,256]{1,0:T(8,128)S(1)}, u32[]{:S(2)}, u32[]{:S(2)}) collective-permute-start(f32[512,256]{1,0:T(8,128)S(1)} %bitcast.129), channel_id=1, source_target_pairs={{0,26},{2,28},{4,30},{6,0},{8,2},{10,4},{12,6},{14,8},{16,10},{18,... | collective-permute-start | bytes 1572872 | tf_op jit(solution)/shard_map/ppermute | solution.py:15
  73.3 1.8 collective-permute-start.1
  75.1 1.3 collective-permute-start
  76.7 9.0 %collective-permute-done.2 = f32[512,256]{1,0:T(8,128)S(1)} collective-permute-done((f32[512,256]{1,0:T(8,128)S(1)}, f32[512,256]{1,0:T(8,128)S(1)}, u32[]{:S(2)}, u32[]{:S(2)}) %collective-permute-start.2) | collective-permute-done | bytes 524320 | tf_op jit(solution)/shard_map/ppermute | solution.py:15
  85.7 6.2 %collective-permute-start.5 = (f32[256,512]{1,0:T(8,128)S(1)}, f32[256,512]{1,0:T(8,128)}, u32[]{:S(2)}, u32[]{:S(2)}) collective-permute-start(f32[256,512]{1,0:T(8,128)S(1)} %copy-done.8), channel_id=1, source_target_pairs={{0,26},{2,28},{4,30},{6,0},{8,2},{10,4},{12,6},{14,8},{16,10},{18,... | collective-permute-start | bytes 1572872 | tf_op jit(solution)/shard_map/ppermute | solution.py:15
  91.9 4.9 %collective-permute-done.1 = f32[512,256]{1,0:T(8,128)S(1)} collective-permute-done((f32[512,256]{1,0:T(8,128)S(1)}, f32[512,256]{1,0:T(8,128)S(1)}, u32[]{:S(2)}, u32[]{:S(2)}) %collective-permute-start.1) | collective-permute-done | bytes 524320 | tf_op jit(solution)/shard_map/ppermute | solution.py:15
  96.8 3.1 %collective-permute-done = f32[512,256]{1,0:T(8,128)S(1)} collective-permute-done((f32[512,256]{1,0:T(8,128)S(1)}, f32[512,256]{1,0:T(8,128)S(1)}, u32[]{:S(2)}, u32[]{:S(2)}) %collective-permute-start) | collective-permute-done | bytes 524320 | tf_op jit(solution)/shard_map/ppermute | solution.py:15
  100.2 14.3 %while.10 = (s32[]{:T(128)}, f32[4,256,256]{2,1,0:T(8,128)}, s32[4,2]{0,1:T(2,128)S(1)}, f32[512,1024]{1,0:T(8,128)S(1)}, s32[]{:T(128)}, /*index=5*/s32[1,1]{0,1:T(1,128)}, s32[]{:T(128)}, s32[]{:T(128)}) while((s32[]{:T(128)}, f32[4,256,256]{2,1,0:T(8,128)}, s32[4,2]{0,1:T(2,128)S(1)}, f32[512,1024]{1,0:T(8,128)S(1)}, s32[]{:T(128)}, ...), condition=%wide.region_1.2_spmd, body=%wide.region_0.1_spmd.sunk | while | flops 402653184 | bytes 1310953 | solution.py:75
  102.1 1.7 fusion.79
  105.6 1.7 fusion.79
  109.2 1.8 fusion.79
  112.8 1.8 fusion.79
  114.6 2.4 broadcast_multiply_fusion
  117.1 4.5 %collective-permute-done.5 = f32[256,512]{1,0:T(8,128)} collective-permute-done((f32[256,512]{1,0:T(8,128)S(1)}, f32[256,512]{1,0:T(8,128)}, u32[]{:S(2)}, u32[]{:S(2)}) %collective-permute-start.5) | collective-permute-done | bytes 524320 | tf_op jit(solution)/shard_map/ppermute | solution.py:15
  121.5 1.6 pad_maximum_fusion.1
  123.1 2.0 gather_fusion.1
  125.1 2.0 gather_fusion
  127.2 25.9 %all-reduce.2.cloned.1.call-done = f32[4,256,256]{2,1,0:T(8,128)} async-done(((f32[4,256,256]{2,1,0:T(8,128)}), f32[4,256,256]{2,1,0:T(8,128)}) %all-reduce.2.cloned.1.call-update) | async-done | bytes 1048592 | tf_op jit(solution)/shard_map/psum | solution.py:77
  153.0 4.2 %fusion.14 = f32[4,256,512]{2,1,0:T(8,128)S(1)} fusion(f32[4,256,256]{2,1,0:T(8,128)} %all-reduce.2.cloned.1.call-done, f32[4,256,512]{2,1,0:T(8,128)} %gather_fusion.1, pred[4]{0:T(512)(128)(4,1)S(1)} %compare_and_fusion), kind=kOutput, calls=%fused_computation.26 | convolution fusion | flops 1611137024 | bytes 5242884 | tf_op jit(solution)/shard_map/pab,pac->pbc/dot_general | solution.py:95
  157.3 3.3 %fusion.7 = f32[4,256,512]{2,0,1:T(4,128)S(1)} fusion(f32[4,256,512]{2,1,0:T(8,128)S(1)} %fusion.14, f32[4]{0:T(128)S(1)} %get-tuple-element.39, s32[4]{0:T(128)S(1)} %bitcast.138), kind=kOutput, calls=%fused_computation.18 | convolution fusion | flops 25690128 | bytes 4194336 | tf_op jit(solution)/shard_map/pl,pac->lac/dot_general | solution.py:110
  160.6 2.1 fusion.16
  162.7 3.8 %fusion.18 = f32[4,256,512]{2,0,1:T(4,128)S(1)} fusion(f32[4,256,512]{2,0,1:T(4,128)S(1)} %fusion.7, f32[4,256,512]{2,1,0:T(8,128)S(1)} %fusion.16, s32[4]{0:T(128)S(1)} %bitcast.136), kind=kOutput, calls=%fused_computation.30 | convolution fusion | flops 25690128 | bytes 6291472 | tf_op jit(solution)/shard_map/pl,pac->lac/dot_general | solution.py:103
  166.5 1.5 fusion.67
  168.2 1.5 collective-permute-start.7
  169.7 1.5 collective-permute-start.8
  171.2 2.4 collective-permute-start.6
  173.6 19.0 %collective-permute-done.7 = f32[256,512]{1,0:T(8,128)S(1)} collective-permute-done((f32[256,512]{1,0:T(8,128)S(1)}, f32[256,512]{1,0:T(8,128)S(1)}, u32[]{:S(2)}, u32[]{:S(2)}) %collective-permute-start.7) | collective-permute-done | bytes 524320 | tf_op jit(solution)/shard_map/ppermute | solution.py:15
  192.6 3.7 %collective-permute-done.8 = f32[256,512]{1,0:T(8,128)S(1)} collective-permute-done((f32[256,512]{1,0:T(8,128)S(1)}, f32[256,512]{1,0:T(8,128)S(1)}, u32[]{:S(2)}, u32[]{:S(2)}) %collective-permute-start.8) | collective-permute-done | bytes 524320 | tf_op jit(solution)/shard_map/ppermute | solution.py:15
  196.7 3.7 %collective-permute-start.11 = (f32[256,512]{1,0:T(8,128)S(1)}, f32[256,512]{1,0:T(8,128)S(1)}, u32[]{:S(2)}, u32[]{:S(2)}) collective-permute-start(f32[256,512]{1,0:T(8,128)S(1)} %fusion.45), channel_id=1, source_target_pairs={{0,26},{2,28},{4,30},{6,0},{8,2},{10,4},{12,6},{14,8},{16,10},{18,... | collective-permute-start | bytes 1572872 | tf_op jit(solution)/shard_map/ppermute | solution.py:15
  200.3 11.5 %collective-permute-start.10 = (f32[256,512]{1,0:T(8,128)S(1)}, f32[256,512]{1,0:T(8,128)S(1)}, u32[]{:S(2)}, u32[]{:S(2)}) collective-permute-start(f32[256,512]{1,0:T(8,128)S(1)} %fusion.45), channel_id=1, source_target_pairs={{0,28},{2,30},{4,0},{6,2},{8,4},{10,6},{12,8},{14,10},{16,12},{18,... | collective-permute-start | bytes 1572872 | tf_op jit(solution)/shard_map/ppermute | solution.py:15
  211.9 9.5 %collective-permute-done.11 = f32[256,512]{1,0:T(8,128)S(1)} collective-permute-done((f32[256,512]{1,0:T(8,128)S(1)}, f32[256,512]{1,0:T(8,128)S(1)}, u32[]{:S(2)}, u32[]{:S(2)}) %collective-permute-start.11) | collective-permute-done | bytes 524320 | tf_op jit(solution)/shard_map/ppermute | solution.py:15
  221.3 12.0 %collective-permute-done.10 = f32[256,512]{1,0:T(8,128)S(1)} collective-permute-done((f32[256,512]{1,0:T(8,128)S(1)}, f32[256,512]{1,0:T(8,128)S(1)}, u32[]{:S(2)}, u32[]{:S(2)}) %collective-permute-start.10) | collective-permute-done | bytes 524320 | tf_op jit(solution)/shard_map/ppermute | solution.py:15
  233.5 2.0 gather_fusion.3
  235.6 2.0 gather_fusion.2
  237.6 4.0 %fusion.10 = f32[4,256,512]{2,1,0:T(8,128)S(1)} fusion(f32[4,256,256]{2,1,0:T(8,128)S(1)} %copy-done.1, f32[4,256,512]{2,1,0:T(8,128)} %gather_fusion.3, pred[4]{0:T(512)(128)(4,1)S(1)} %compare_and_fusion), kind=kOutput, calls=%fused_computation.22 | convolution fusion | flops 1611137024 | bytes 5242884 | tf_op jit(solution)/shard_map/pab,pac->pbc/dot_general | solution.py:95
  241.5 3.3 %fusion.4 = f32[4,256,512]{2,0,1:T(4,128)S(1)} fusion(f32[4,256,512]{2,1,0:T(8,128)S(1)} %fusion.10, f32[4]{0:T(128)S(1)} %get-tuple-element.39, s32[4]{0:T(128)S(1)} %bitcast.139), kind=kOutput, calls=%fused_computation.14 | convolution fusion | flops 25690128 | bytes 4194336 | tf_op jit(solution)/shard_map/pl,pac->lac/dot_general | solution.py:110
  244.9 2.1 fusion.12
  247.0 3.2 %fusion.5 = f32[4,256,512]{2,0,1:T(4,128)S(1)} fusion(f32[4,256,512]{2,1,0:T(8,128)S(1)} %fusion.12, s32[4]{0:T(128)S(1)} %bitcast.137), kind=kOutput, calls=%fused_computation.15 | convolution fusion | flops 25165840 | bytes 4194320 | tf_op jit(solution)/shard_map/pl,pac->lac/dot_general | solution.py:103
  250.3 1.2 copy_add_fusion
  251.6 1.6 collective-permute-start.12
  253.2 7.3 %collective-permute-start.14 = (f32[256,512]{1,0:T(8,128)S(1)}, f32[256,512]{1,0:T(8,128)S(1)}, u32[]{:S(2)}, u32[]{:S(2)}) collective-permute-start(f32[256,512]{1,0:T(8,128)S(1)} %get-tuple-element.44), channel_id=1, source_target_pairs={{0,6},{2,8},{4,10},{6,12},{8,14},{10,16},{12,18},{14,20},{16,22},{... | collective-permute-start | bytes 1572872 | tf_op jit(solution)/shard_map/ppermute | solution.py:15
  260.5 4.8 %collective-permute-start.13 = (f32[256,512]{1,0:T(8,128)S(1)}, f32[256,512]{1,0:T(8,128)S(1)}, u32[]{:S(2)}, u32[]{:S(2)}) collective-permute-start(f32[256,512]{1,0:T(8,128)S(1)} %get-tuple-element.45), channel_id=1, source_target_pairs={{0,4},{2,6},{4,8},{6,10},{8,12},{10,14},{12,16},{14,18},{16,20},{1... | collective-permute-start | bytes 1572872 | tf_op jit(solution)/shard_map/ppermute | solution.py:15
  265.3 8.8 %collective-permute-done.12 = f32[256,512]{1,0:T(8,128)S(1)} collective-permute-done((f32[256,512]{1,0:T(8,128)S(1)}, f32[256,512]{1,0:T(8,128)S(1)}, u32[]{:S(2)}, u32[]{:S(2)}) %collective-permute-start.12) | collective-permute-done | bytes 524320 | tf_op jit(solution)/shard_map/ppermute | solution.py:15
  274.1 6.1 %collective-permute-done.14 = f32[256,512]{1,0:T(8,128)S(1)} collective-permute-done((f32[256,512]{1,0:T(8,128)S(1)}, f32[256,512]{1,0:T(8,128)S(1)}, u32[]{:S(2)}, u32[]{:S(2)}) %collective-permute-start.14) | collective-permute-done | bytes 524320 | tf_op jit(solution)/shard_map/ppermute | solution.py:15
  280.2 19.1 %collective-permute-done.13 = f32[256,512]{1,0:T(8,128)S(1)} collective-permute-done((f32[256,512]{1,0:T(8,128)S(1)}, f32[256,512]{1,0:T(8,128)S(1)}, u32[]{:S(2)}, u32[]{:S(2)}) %collective-permute-start.13) | collective-permute-done | bytes 524320 | tf_op jit(solution)/shard_map/ppermute | solution.py:15
  (57 shorter events, 5.9 us)
Async XLA Ops:
  6.5 69.9 %copy-start = (f32[8]{0:T(128)S(1)}, f32[8]{0:T(128)}, u32[]{:S(2)}) copy-start(f32[8]{0:T(128)} %param.14) | copy-start | bytes 100
  6.5 29.4 %copy-start.8 = (f32[256,512]{1,0:T(8,128)S(1)}, f32[256,512]{1,0:T(8,128)}, u32[]{:S(2)}) copy-start(f32[256,512]{1,0:T(8,128)} %param.17) | copy-start | bytes 1572868
  6.5 35.5 %copy-start.9 = (s32[4,3]{1,0:T(4,128)S(1)}, s32[4,3]{1,0:T(4,128)}, u32[]{:S(2)}) copy-start(s32[4,3]{1,0:T(4,128)} %param.12) | copy-start | bytes 148
  28.6 21.4 %all-to-all-start = ((f32[16,32,256]{2,1,0:T(8,128)}), f32[16,32,256]{2,1,0:T(8,128)S(1)}, u32[]{:S(2)}, u32[]{:S(2)}) async-start(f32[16,32,256]{2,1,0:T(8,128)} %constant_dynamic-update-slice_fusion), calls=%async_computation | async-start | bytes 1048576 | tf_op jit(solution)/shard_map/all_to_all | solution.py:41
  35.9 117.2 %all-reduce.2.cloned.1.call-start = ((), (), s32[]{:S(2)}) async-start(), calls=%async_computation.1 | async-start | bytes 2097152 | tf_op jit(solution)/shard_map/psum | solution.py:77
  35.9 81.1 %collective-permute-start.4 = (f32[256,512]{1,0:T(8,128)S(1)}, f32[256,512]{1,0:T(8,128)}, u32[]{:S(2)}, u32[]{:S(2)}) collective-permute-start(f32[256,512]{1,0:T(8,128)S(1)} %copy-done.8), channel_id=1, source_target_pairs={{0,28},{2,30},{4,0},{6,2},{8,4},{10,6},{12,8},{14,10},{16,12},{18,... | collective-permute-start | bytes 1572872 | tf_op jit(solution)/shard_map/ppermute | solution.py:15
  40.2 76.9 %collective-permute-start.3 = (f32[256,512]{1,0:T(8,128)S(1)}, f32[256,512]{1,0:T(8,128)}, u32[]{:S(2)}, u32[]{:S(2)}) collective-permute-start(f32[256,512]{1,0:T(8,128)S(1)} %copy-done.8), channel_id=1, source_target_pairs={{0,30},{2,0},{4,2},{6,4},{8,6},{10,8},{12,10},{14,12},{16,14},{18,... | collective-permute-start | bytes 1572872 | tf_op jit(solution)/shard_map/ppermute | solution.py:15
  50.0 35.7 %collective-permute-start.2 = (f32[512,256]{1,0:T(8,128)S(1)}, f32[512,256]{1,0:T(8,128)S(1)}, u32[]{:S(2)}, u32[]{:S(2)}) collective-permute-start(f32[512,256]{1,0:T(8,128)S(1)} %bitcast.129), channel_id=1, source_target_pairs={{0,26},{2,28},{4,30},{6,0},{8,2},{10,4},{12,6},{14,8},{16,10},{18,... | collective-permute-start | bytes 1572872 | tf_op jit(solution)/shard_map/ppermute | solution.py:15
  73.3 23.5 %collective-permute-start.1 = (f32[512,256]{1,0:T(8,128)S(1)}, f32[512,256]{1,0:T(8,128)S(1)}, u32[]{:S(2)}, u32[]{:S(2)}) collective-permute-start(f32[512,256]{1,0:T(8,128)S(1)} %bitcast.130), channel_id=1, source_target_pairs={{0,28},{2,30},{4,0},{6,2},{8,4},{10,6},{12,8},{14,10},{16,12},{18,... | collective-permute-start | bytes 1572872 | tf_op jit(solution)/shard_map/ppermute | solution.py:15
  75.1 24.8 %collective-permute-start = (f32[512,256]{1,0:T(8,128)S(1)}, f32[512,256]{1,0:T(8,128)S(1)}, u32[]{:S(2)}, u32[]{:S(2)}) collective-permute-start(f32[512,256]{1,0:T(8,128)S(1)} %bitcast.131), channel_id=1, source_target_pairs={{0,30},{2,0},{4,2},{6,4},{8,6},{10,8},{12,10},{14,12},{16,14},{18,... | collective-permute-start | bytes 1572872 | tf_op jit(solution)/shard_map/ppermute | solution.py:15
  85.7 35.9 %collective-permute-start.5 = (f32[256,512]{1,0:T(8,128)S(1)}, f32[256,512]{1,0:T(8,128)}, u32[]{:S(2)}, u32[]{:S(2)}) collective-permute-start(f32[256,512]{1,0:T(8,128)S(1)} %copy-done.8), channel_id=1, source_target_pairs={{0,26},{2,28},{4,30},{6,0},{8,2},{10,4},{12,6},{14,8},{16,10},{18,... | collective-permute-start | bytes 1572872 | tf_op jit(solution)/shard_map/ppermute | solution.py:15
  157.2 3.4 %copy-start.1 = (f32[4,256,256]{2,1,0:T(8,128)S(1)}, f32[4,256,256]{2,1,0:T(8,128)}, u32[]{:S(2)}) copy-start(f32[4,256,256]{2,1,0:T(8,128)} %all-reduce.2.cloned.1.call-done) | copy-start | bytes 3145732
  157.2 3.4 %copy-start.2 = (f32[4,256,512]{2,1,0:T(8,128)S(1)}, f32[4,256,512]{2,1,0:T(8,128)}, u32[]{:S(2)}) copy-start(f32[4,256,512]{2,1,0:T(8,128)} %gather_fusion) | copy-start | bytes 6291460
  168.1 28.2 %copy-start.6 = (f32[256,512]{1,0:T(8,128)S(1)}, f32[256,512]{1,0:T(8,128)}, u32[]{:S(2)}) copy-start(f32[256,512]{1,0:T(8,128)} %param.16) | copy-start | bytes 1572868
  168.2 24.4 %collective-permute-start.7 = (f32[256,512]{1,0:T(8,128)S(1)}, f32[256,512]{1,0:T(8,128)S(1)}, u32[]{:S(2)}, u32[]{:S(2)}) collective-permute-start(f32[256,512]{1,0:T(8,128)S(1)} %bitcast.135), channel_id=1, source_target_pairs={{0,4},{2,6},{4,8},{6,10},{8,12},{10,14},{12,16},{14,18},{16,20},{1... | collective-permute-start | bytes 1572872 | tf_op jit(solution)/shard_map/ppermute | solution.py:15
  169.7 26.6 %collective-permute-start.8 = (f32[256,512]{1,0:T(8,128)S(1)}, f32[256,512]{1,0:T(8,128)S(1)}, u32[]{:S(2)}, u32[]{:S(2)}) collective-permute-start(f32[256,512]{1,0:T(8,128)S(1)} %bitcast.134), channel_id=1, source_target_pairs={{0,6},{2,8},{4,10},{6,12},{8,14},{10,16},{12,18},{14,20},{16,22},{... | collective-permute-start | bytes 1572872 | tf_op jit(solution)/shard_map/ppermute | solution.py:15
  171.2 25.1 %collective-permute-start.6 = (f32[256,512]{1,0:T(8,128)S(1)}, f32[256,512]{1,0:T(8,128)S(1)}, u32[]{:S(2)}, u32[]{:S(2)}) collective-permute-start(f32[256,512]{1,0:T(8,128)S(1)} %bitcast.133), channel_id=1, source_target_pairs={{0,2},{2,4},{4,6},{6,8},{8,10},{10,12},{12,14},{14,16},{16,18},{18... | collective-permute-start | bytes 1572872 | tf_op jit(solution)/shard_map/ppermute | solution.py:15
  196.7 36.9 %copy-start.4 = (f32[256,512]{1,0:T(8,128)}, f32[256,512]{1,0:T(8,128)S(1)}, u32[]{:S(2)}) copy-start(f32[256,512]{1,0:T(8,128)S(1)} %fusion.45) | copy-start | bytes 1572868
  196.7 24.7 %collective-permute-start.11 = (f32[256,512]{1,0:T(8,128)S(1)}, f32[256,512]{1,0:T(8,128)S(1)}, u32[]{:S(2)}, u32[]{:S(2)}) collective-permute-start(f32[256,512]{1,0:T(8,128)S(1)} %fusion.45), channel_id=1, source_target_pairs={{0,26},{2,28},{4,30},{6,0},{8,2},{10,4},{12,6},{14,8},{16,10},{18,... | collective-permute-start | bytes 1572872 | tf_op jit(solution)/shard_map/ppermute | solution.py:15
  200.3 33.0 %collective-permute-start.10 = (f32[256,512]{1,0:T(8,128)S(1)}, f32[256,512]{1,0:T(8,128)S(1)}, u32[]{:S(2)}, u32[]{:S(2)}) collective-permute-start(f32[256,512]{1,0:T(8,128)S(1)} %fusion.45), channel_id=1, source_target_pairs={{0,28},{2,30},{4,0},{6,2},{8,4},{10,6},{12,8},{14,10},{16,12},{18,... | collective-permute-start | bytes 1572872 | tf_op jit(solution)/shard_map/ppermute | solution.py:15
  211.8 21.5 %collective-permute-start.9 = (f32[256,512]{1,0:T(8,128)S(1)}, f32[256,512]{1,0:T(8,128)S(1)}, u32[]{:S(2)}, u32[]{:S(2)}) collective-permute-start(f32[256,512]{1,0:T(8,128)S(1)} %fusion.45), channel_id=1, source_target_pairs={{0,30},{2,0},{4,2},{6,4},{8,6},{10,8},{12,10},{14,12},{16,14},{18,... | collective-permute-start | bytes 1572872 | tf_op jit(solution)/shard_map/ppermute | solution.py:15
  241.5 3.4 %copy-start.3 = (f32[4,256,512]{2,1,0:T(8,128)S(1)}, f32[4,256,512]{2,1,0:T(8,128)}, u32[]{:S(2)}) copy-start(f32[4,256,512]{2,1,0:T(8,128)} %gather_fusion.2) | copy-start | bytes 6291460
  251.5 47.8 %copy-start.5 = (f32[256,512]{1,0:T(8,128)S(1)}, f32[256,512]{1,0:T(8,128)}, u32[]{:S(2)}) copy-start(f32[256,512]{1,0:T(8,128)} %copy-done.4) | copy-start | bytes 1572868
  251.5 47.8 %copy-start.7 = (f32[256,512]{1,0:T(8,128)S(1)}, f32[256,512]{1,0:T(8,128)}, u32[]{:S(2)}) copy-start(f32[256,512]{1,0:T(8,128)} %param.16) | copy-start | bytes 1572868
  251.6 22.4 %collective-permute-start.12 = (f32[256,512]{1,0:T(8,128)S(1)}, f32[256,512]{1,0:T(8,128)S(1)}, u32[]{:S(2)}, u32[]{:S(2)}) collective-permute-start(f32[256,512]{1,0:T(8,128)S(1)} %get-tuple-element.43), channel_id=1, source_target_pairs={{0,2},{2,4},{4,6},{6,8},{8,10},{10,12},{12,14},{14,16},{16,18},{18... | collective-permute-start | bytes 1572872 | tf_op jit(solution)/shard_map/ppermute | solution.py:15
  253.2 27.0 %collective-permute-start.14 = (f32[256,512]{1,0:T(8,128)S(1)}, f32[256,512]{1,0:T(8,128)S(1)}, u32[]{:S(2)}, u32[]{:S(2)}) collective-permute-start(f32[256,512]{1,0:T(8,128)S(1)} %get-tuple-element.44), channel_id=1, source_target_pairs={{0,6},{2,8},{4,10},{6,12},{8,14},{10,16},{12,18},{14,20},{16,22},{... | collective-permute-start | bytes 1572872 | tf_op jit(solution)/shard_map/ppermute | solution.py:15
  260.5 38.8 %collective-permute-start.13 = (f32[256,512]{1,0:T(8,128)S(1)}, f32[256,512]{1,0:T(8,128)S(1)}, u32[]{:S(2)}, u32[]{:S(2)}) collective-permute-start(f32[256,512]{1,0:T(8,128)S(1)} %get-tuple-element.45), channel_id=1, source_target_pairs={{0,4},{2,6},{4,8},{6,10},{8,12},{10,14},{12,16},{14,18},{16,20},{1... | collective-permute-start | bytes 1572872 | tf_op jit(solution)/shard_map/ppermute | solution.py:15
Sparse Core Ops, SparseCore 0:
  117.1 35.9 all-reduce.1
